TPU v7x, 32 devices: a whole 2x2x4 slice. The times are simulated.
32 devices in a mesh: batch: 4 (over y, core), blk: 8 (over z, x).
Axes of the slice: x: 2, y: 2, z: 4, core: 2. Of those that a mesh axis runs over, the one named last changes fastest.
Arguments:
- inputs: bfloat16 [2, 4, 1024, 1024], P(None, 'batch', 'blk'), may hold values from -6 to 6
- segment_ids: int32 [2, 4, 1024], P(None, 'batch', 'blk'), may hold values from 0 to 3, never falling along the last dimension, each value on 1 to 640 neighbouring positions
- cotangent: bfloat16 [2, 4, 1024, 1024], P(None, 'batch', 'blk'), may hold values from -6 to 6
- qkv_weight: bfloat16 [1024, 3072], P(('batch', 'blk')), may hold values from -0.1875 to 0.1875
- out_weight: bfloat16 [1024, 1024], P(('batch', 'blk')), may hold values from -0.75 to 0.75
- up_weight: bfloat16 [1024, 4096], P(('batch', 'blk')), may hold values from -0.1875 to 0.1875
- down_weight: bfloat16 [4096, 1024], P(('batch', 'blk')), may hold values from -0.09375 to 0.09375
- first_gain: bfloat16 [1024], P(('batch', 'blk')), may hold values from 0.5 to 1.5
- first_bias: bfloat16 [1024], P(('batch', 'blk')), may hold values from -4 to 4
- second_gain: bfloat16 [1024], P(('batch', 'blk')), may hold values from 0.5 to 1.5
- second_bias: bfloat16 [1024], P(('batch', 'blk')), may hold values from -4 to 4
- out_bias: bfloat16 [1024], P(('batch', 'blk')), may hold values from -4 to 4
- up_bias: bfloat16 [4096], P(('batch', 'blk')), may hold values from -4 to 4
- down_bias: bfloat16 [1024], P(('batch', 'blk')), may hold values from -4 to 4
Outputs:
- result: float32 [2, 4, 1024, 1024], P(None, 'batch', 'blk')
- input_grad: float32 [2, 4, 1024, 1024], P(None, 'batch', 'blk')
- qkv_grad: float32 [1024, 3072], P(('batch', 'blk'))
- out_grad: float32 [1024, 1024], P(('batch', 'blk'))
- up_grad: float32 [1024, 4096], P(('batch', 'blk'))
- down_grad: float32 [4096, 1024], P(('batch', 'blk'))
- first_gain_grad: float32 [1024], P(('batch', 'blk'))
- first_bias_grad: float32 [1024], P(('batch', 'blk'))
- second_gain_grad: float32 [1024], P(('batch', 'blk'))
- second_bias_grad: float32 [1024], P(('batch', 'blk'))
- out_bias_grad: float32 [1024], P(('batch', 'blk'))
- up_bias_grad: float32 [4096], P(('batch', 'blk'))
- down_bias_grad: float32 [1024], P(('batch', 'blk'))
Inputs may be any that keep to these rules, and one draw needn't show every extreme that they name: `segment_ids`: along each set the ids never fall; each image holds 1 to 640 latents, and one image of every set holds exactly 640.
All inputs are finite; a program needn't handle non-finite values.
Results may differ from a plain program's by a relative error of at most 0.025.
Values may be sent and summed in bfloat16 or wider, within the bound.
No kernel may reach another device: no remote copies, remote signals or barrier semaphores. Data moves between devices by JAX's collectives and lax.ppermute only.
A program may use at most 320 MiB of HBM per device.

v0:
```python
from functools import partial

import jax
import jax.numpy as jnp
from jax import lax
from jax.sharding import PartitionSpec as P

H = 8


epsilon = 1e-05
masked_score = -1e30


def dense(former, latter):
    return jnp.dot(former, latter, preferred_element_type=jnp.float32)


def norm_rows(values, gains, shifts):
    average = jnp.mean(values, axis=-1, keepdims=True)
    centred = values - average
    inverse = lax.rsqrt(jnp.mean(centred * centred, axis=-1, keepdims=True) + epsilon)
    scaled = centred * inverse
    return (scaled * gains + shifts, scaled, inverse)


def norm_back(gradient, scaled, inverse, gains):
    upstream = gradient * gains
    return inverse * (
        upstream
        - jnp.mean(upstream, axis=-1, keepdims=True)
        - scaled * jnp.mean(upstream * scaled, axis=-1, keepdims=True)
    )


def block_scan(update, carried, pieces):
    amount = pieces[0].shape[1]
    stride = min(512, amount)

    def block_step(state_now, number):
        sliced = tuple(
            (lax.dynamic_slice_in_dim(member, number * stride, stride, 1) for member in pieces)
        )
        return (update(state_now, sliced), None)

    carried, unused = lax.scan(block_step, carried, jnp.arange(amount // stride))
    return carried


def split_heads(rows, head_count):
    return rows.reshape(rows.shape[0], rows.shape[1], head_count, rows.shape[2] // head_count)


def attend_piece(running, sliced, queries, query_segs):
    maximum, totals, accumulated = running
    key_part, value_part, seg_part = sliced
    head_count, head_size = (queries.shape[2], queries.shape[3])
    key_heads = split_heads(key_part, head_count)
    value_heads = split_heads(value_part, head_count)
    scores = jnp.einsum(
        "sqhd,skhd->shqk", queries, key_heads, preferred_element_type=jnp.float32
    ) * head_size ** (-0.5)
    allowed = query_segs[:, None, :, None] == seg_part[:, None, None, :]
    scores = jnp.where(allowed, scores, masked_score)
    highest = jnp.maximum(maximum, jnp.max(scores, axis=-1, keepdims=True))
    factor = jnp.exp(maximum - highest)
    shares = jnp.exp(scores - highest)
    totals = totals * factor + jnp.sum(shares, axis=-1, keepdims=True)
    accumulated = accumulated * factor + jnp.einsum(
        "shqk,skhd->shqd",
        shares.astype(jnp.bfloat16),
        value_heads,
        preferred_element_type=jnp.float32,
    )
    return (highest, totals, accumulated)


def fold_keys(running, pieces, queries, query_segs):
    return block_scan(
        partial(attend_piece, queries=queries, query_segs=query_segs), running, pieces
    )


def grad_block(queries, grad_heads, query_segs, log_total, delta, key_heads, value_heads, key_segs):
    head_size = queries.shape[3]
    scores = jnp.einsum(
        "sqhd,skhd->shqk", queries, key_heads, preferred_element_type=jnp.float32
    ) * head_size ** (-0.5)
    allowed = query_segs[:, None, :, None] == key_segs[:, None, None, :]
    shares = jnp.where(allowed, jnp.exp(scores - log_total), 0.0)
    grad_shares = jnp.einsum(
        "sqhd,skhd->shqk", grad_heads, value_heads, preferred_element_type=jnp.float32
    )
    grad_scores = (shares * (grad_shares - delta)).astype(jnp.bfloat16)
    return (shares.astype(jnp.bfloat16), grad_scores)


def micro_step(set_inputs, set_segs, set_cotangent, gathered):
    (
        weight_qkv,
        weight_out,
        weight_up,
        weight_down,
        gain_one,
        shift_one,
        gain_two,
        shift_two,
        bias_out,
        bias_up,
        bias_down,
    ) = gathered
    set_count, tok_count, features = set_inputs.shape
    head_count = H
    head_size = features // head_count
    scale = head_size ** (-0.5)
    rows = set_inputs.astype(jnp.float32).reshape(-1, features)
    normed, scaled_one, inverse_one = norm_rows(
        rows, gain_one.astype(jnp.float32), shift_one.astype(jnp.float32)
    )
    normed_low = normed.astype(jnp.bfloat16)
    mixed = dense(normed_low, weight_qkv).astype(jnp.bfloat16)
    queries = mixed[:, :features].reshape(set_count, tok_count, head_count, head_size)
    key_rows = mixed[:, features : 2 * features].reshape(set_count, tok_count, features)
    value_rows = mixed[:, 2 * features :].reshape(set_count, tok_count, features)
    running = (
        jnp.full((set_count, head_count, tok_count, 1), masked_score, jnp.float32),
        jnp.zeros((set_count, head_count, tok_count, 1), jnp.float32),
        jnp.zeros((set_count, head_count, tok_count, head_size), jnp.float32),
    )
    running = fold_keys(
        running,
        (
            lax.all_gather(key_rows, "blk", axis=1, tiled=True),
            lax.all_gather(value_rows, "blk", axis=1, tiled=True),
            lax.all_gather(set_segs, "blk", axis=1, tiled=True),
        ),
        queries=queries,
        query_segs=set_segs,
    )
    maximum, totals, accumulated = running
    attended = accumulated / totals
    log_total = maximum + jnp.log(totals)
    attended_low = jnp.transpose(attended, (0, 2, 1, 3)).reshape(-1, features).astype(jnp.bfloat16)
    middle = rows + dense(attended_low, weight_out) + bias_out.astype(jnp.float32)
    normed_two, scaled_two, inverse_two = norm_rows(
        middle, gain_two.astype(jnp.float32), shift_two.astype(jnp.float32)
    )
    normed_two_low = normed_two.astype(jnp.bfloat16)
    upper = dense(normed_two_low, weight_up) + bias_up.astype(jnp.float32)
    activ_value, gelu_back = jax.vjp(lambda v: jax.nn.gelu(v, approximate=False), upper)
    activ_low = activ_value.astype(jnp.bfloat16)
    final = middle + dense(activ_low, weight_down) + bias_down.astype(jnp.float32)
    grad_out = set_cotangent.astype(jnp.float32).reshape(-1, features)
    grad_low = grad_out.astype(jnp.bfloat16)
    grad_down_bias = jnp.sum(grad_low.astype(jnp.float32), axis=0)
    grad_down = jnp.einsum("rf,rd->fd", activ_low, grad_low, preferred_element_type=jnp.float32)
    grad_activ = jnp.einsum("rd,fd->rf", grad_low, weight_down, preferred_element_type=jnp.float32)
    grad_upper = gelu_back(grad_activ)[0].astype(jnp.bfloat16)
    grad_up_bias = jnp.sum(grad_upper.astype(jnp.float32), axis=0)
    grad_up = jnp.einsum(
        "rd,rf->df", normed_two_low, grad_upper, preferred_element_type=jnp.float32
    )
    grad_normed_two = jnp.einsum(
        "rf,df->rd", grad_upper, weight_up, preferred_element_type=jnp.float32
    )
    grad_gain_two = jnp.sum(grad_normed_two * scaled_two, axis=0)
    grad_shift_two = jnp.sum(grad_normed_two, axis=0)
    grad_middle = grad_out + norm_back(
        grad_normed_two, scaled_two, inverse_two, gain_two.astype(jnp.float32)
    )
    branch_low = grad_middle.astype(jnp.bfloat16)
    grad_out_bias = jnp.sum(branch_low.astype(jnp.float32), axis=0)
    grad_out_weight = jnp.einsum(
        "rd,re->de", attended_low, branch_low, preferred_element_type=jnp.float32
    )
    grad_attended = jnp.einsum(
        "re,de->rd", branch_low, weight_out, preferred_element_type=jnp.float32
    )
    grad_heads = grad_attended.astype(jnp.bfloat16).reshape(
        set_count, tok_count, head_count, head_size
    )
    delta = jnp.einsum("sqhd,shqd->shq", grad_heads.astype(jnp.float32), attended)[..., None]
    everything = (
        lax.all_gather(key_rows, "blk", axis=1, tiled=True),
        lax.all_gather(value_rows, "blk", axis=1, tiled=True),
        lax.all_gather(set_segs, "blk", axis=1, tiled=True),
    )
    length = everything[0].shape[1]
    stride = min(512, length)

    def key_block(grad_query, number):
        key_part = lax.dynamic_slice_in_dim(everything[0], number * stride, stride, 1)
        value_part = lax.dynamic_slice_in_dim(everything[1], number * stride, stride, 1)
        seg_part = lax.dynamic_slice_in_dim(everything[2], number * stride, stride, 1)
        key_heads = split_heads(key_part, head_count)
        share_low, score_low = grad_block(
            queries,
            grad_heads,
            set_segs,
            log_total,
            delta,
            key_heads,
            split_heads(value_part, head_count),
            seg_part,
        )
        grad_query = (
            grad_query
            + jnp.einsum(
                "shqk,skhd->sqhd", score_low, key_heads, preferred_element_type=jnp.float32
            )
            * scale
        )
        key_term = (
            jnp.einsum("shqk,sqhd->kshd", score_low, queries, preferred_element_type=jnp.float32)
            * scale
        )
        value_term = jnp.einsum(
            "shqk,sqhd->kshd", share_low, grad_heads, preferred_element_type=jnp.float32
        )
        return (
            grad_query,
            jnp.concatenate(
                (
                    key_term.reshape(stride, set_count, features),
                    value_term.reshape(stride, set_count, features),
                ),
                axis=-1,
            ),
        )

    grad_query, terms = lax.scan(
        key_block, jnp.zeros(queries.shape, jnp.float32), jnp.arange(length // stride)
    )
    summed = lax.psum_scatter(
        terms.reshape(length, set_count, 2 * features).astype(jnp.bfloat16),
        "blk",
        scatter_dimension=0,
        tiled=True,
    ).astype(jnp.float32)
    summed = jnp.transpose(summed, (1, 0, 2)).reshape(-1, 2 * features)
    grad_keys = summed[:, :features]
    grad_values = summed[:, features:]
    grad_mixed = jnp.concatenate(
        (grad_query.reshape(-1, features), grad_keys, grad_values), axis=-1
    ).astype(jnp.bfloat16)
    grad_qkv = jnp.einsum("rd,re->de", normed_low, grad_mixed, preferred_element_type=jnp.float32)
    grad_normed = jnp.einsum(
        "re,de->rd", grad_mixed, weight_qkv, preferred_element_type=jnp.float32
    )
    grad_gain_one = jnp.sum(grad_normed * scaled_one, axis=0)
    grad_shift_one = jnp.sum(grad_normed, axis=0)
    grad_input = grad_middle + norm_back(
        grad_normed, scaled_one, inverse_one, gain_one.astype(jnp.float32)
    )
    local_grads = (
        grad_qkv,
        grad_out_weight,
        grad_up,
        grad_down,
        grad_gain_one,
        grad_shift_one,
        grad_gain_two,
        grad_shift_two,
        grad_out_bias,
        grad_up_bias,
        grad_down_bias,
    )
    return (
        final.reshape(set_count, tok_count, features),
        grad_input.reshape(set_count, tok_count, features),
        local_grads,
    )


def body(
    inputs,
    segment_ids,
    cotangent,
    qkv_weight,
    out_weight,
    up_weight,
    down_weight,
    first_gain,
    first_bias,
    second_gain,
    second_bias,
    out_bias,
    up_bias,
    down_bias,
):
    shards = (
        qkv_weight,
        out_weight,
        up_weight,
        down_weight,
        first_gain,
        first_bias,
        second_gain,
        second_bias,
        out_bias,
        up_bias,
        down_bias,
    )
    shard_sums = tuple((jnp.zeros(member.shape, jnp.float32) for member in shards))
    outcomes = []
    input_grads = []
    for micro_index in range(inputs.shape[0]):
        gathered = (
            lax.all_gather(qkv_weight, ("batch", "blk"), axis=0, tiled=True),
            lax.all_gather(out_weight, ("batch", "blk"), axis=0, tiled=True),
            lax.all_gather(up_weight, ("batch", "blk"), axis=0, tiled=True),
            lax.all_gather(down_weight, ("batch", "blk"), axis=0, tiled=True),
            lax.all_gather(first_gain, ("batch", "blk"), axis=0, tiled=True),
            lax.all_gather(first_bias, ("batch", "blk"), axis=0, tiled=True),
            lax.all_gather(second_gain, ("batch", "blk"), axis=0, tiled=True),
            lax.all_gather(second_bias, ("batch", "blk"), axis=0, tiled=True),
            lax.all_gather(out_bias, ("batch", "blk"), axis=0, tiled=True),
            lax.all_gather(up_bias, ("batch", "blk"), axis=0, tiled=True),
            lax.all_gather(down_bias, ("batch", "blk"), axis=0, tiled=True),
        )
        final, grad_input, local_grads = micro_step(
            inputs[micro_index], segment_ids[micro_index], cotangent[micro_index], gathered
        )
        outcomes.append(final)
        input_grads.append(grad_input)
        summed = (
            lax.psum_scatter(local_grads[0], ("batch", "blk"), scatter_dimension=0, tiled=True),
            lax.psum_scatter(local_grads[1], ("batch", "blk"), scatter_dimension=0, tiled=True),
            lax.psum_scatter(local_grads[2], ("batch", "blk"), scatter_dimension=0, tiled=True),
            lax.psum_scatter(local_grads[3], ("batch", "blk"), scatter_dimension=0, tiled=True),
            lax.psum_scatter(local_grads[4], ("batch", "blk"), scatter_dimension=0, tiled=True),
            lax.psum_scatter(local_grads[5], ("batch", "blk"), scatter_dimension=0, tiled=True),
            lax.psum_scatter(local_grads[6], ("batch", "blk"), scatter_dimension=0, tiled=True),
            lax.psum_scatter(local_grads[7], ("batch", "blk"), scatter_dimension=0, tiled=True),
            lax.psum_scatter(local_grads[8], ("batch", "blk"), scatter_dimension=0, tiled=True),
            lax.psum_scatter(local_grads[9], ("batch", "blk"), scatter_dimension=0, tiled=True),
            lax.psum_scatter(local_grads[10], ("batch", "blk"), scatter_dimension=0, tiled=True),
        )
        shard_sums = tuple((former + latter for former, latter in zip(shard_sums, summed)))
    return (jnp.stack(outcomes), jnp.stack(input_grads)) + tuple(shard_sums)


def solution(mesh):
    return jax.shard_map(
        body,
        mesh=mesh,
        in_specs=(
            P(None, "batch", "blk", None),
            P(None, "batch", "blk"),
            P(None, "batch", "blk", None),
            P(("batch", "blk"), None),
            P(("batch", "blk"), None),
            P(("batch", "blk"), None),
            P(("batch", "blk"), None),
            P(("batch", "blk")),
            P(("batch", "blk")),
            P(("batch", "blk")),
            P(("batch", "blk")),
            P(("batch", "blk")),
            P(("batch", "blk")),
            P(("batch", "blk")),
        ),
        out_specs=(
            P(None, "batch", "blk", None),
            P(None, "batch", "blk", None),
            P(("batch", "blk"), None),
            P(("batch", "blk"), None),
            P(("batch", "blk"), None),
            P(("batch", "blk"), None),
            P(("batch", "blk")),
            P(("batch", "blk")),
            P(("batch", "blk")),
            P(("batch", "blk")),
            P(("batch", "blk")),
            P(("batch", "blk")),
            P(("batch", "blk")),
        ),
        check_vma=False,
    )
```

profile of v0, /device:TPU:0, one launch (start us, length us, event | category | flops | bytes accessed | tf_op | source)
XLA Modules:
  0.0 1784.3 jit_solution(10907326481993105442)
XLA Ops:
  13.0 42.4 %all-reduce.14 = (bf16[1024]{0:T(1024)(128)(2,1)S(1)}, bf16[1024]{0:T(1024)(128)(2,1)S(1)}, bf16[1024]{0:T(1024)(128)(2,1)S(1)}, bf16[1024]{0:T(1024)(128)(2,1)}...) all-reduce(bf16[1024]{0:T(1024)(128)(2,1)S(1)} %dynamic-update-slic, ...), channel_id=1, replica_groups=mesh['batch'=4,'blk'=8] {'batch','blk'}, use_global_device_ids=true, to_apply=%add.1 | all-reduce | flops 6144 | bytes 24576
  58.0 25.4 %all-gather.16.cloned.1.call-done = bf16[1024,3072]{1,0:T(8,128)(2,1)} async-done(((bf16[32,3072]{1,0:T(8,128)(2,1)}), bf16[1024,3072]{1,0:T(8,128)(2,1)}) %all-gather.16.cloned.1.call-update) | async-done | bytes 6291472 | tf_op jit(solution)/shard_map/all_gather | solution.py:309
  96.7 65.8 %all-gather.6 = bf16[32,1,128]{2,1,0:T(2,128)(2,1)S(1)} all-gather(bf16[1,1,128]{2,1,0:T(2,128)(2,1)S(1)} %bitcast.544), channel_id=1, replica_groups=mesh['batch'=4,'blk'=8] {'batch','blk'}, dimensions={0}, use_global_device_ids=true | all-gather | bytes 8448 | tf_op jit(solution)/shard_map/all_gather | solution.py:318
  162.6 16.3 all-gather.3
  178.9 18.6 %all-gather = s32[1,1,1024]{2,1,0:T(1,128)S(1)} all-gather(s32[1,1,128]{2,1,0:T(1,128)S(1)} %get-tuple-element.1147), channel_id=2, replica_groups=mesh['batch'=4,'blk'=8] {'blk'}, dimensions={2}, use_global_device_ids=true | all-gather | bytes 4608 | tf_op jit(solution)/shard_map/all_gather | solution.py:135
  207.9 12.6 while.57
  222.5 14.3 all-gather.24.cloned.1.call-done
  240.8 45.8 %all-gather.26.cloned.1.call-done = bf16[1024,1024]{1,0:T(8,128)(2,1)} async-done(((bf16[128,1024]{1,0:T(8,128)(2,1)}), bf16[1024,1024]{1,0:T(8,128)(2,1)}) %all-gather.26.cloned.1.call-update) | async-done | bytes 2097168 | tf_op jit(solution)/shard_map/all_gather | solution.py:134
  290.6 12.4 while.56
  305.6 39.0 %all-gather.18.cloned.1.call-done = bf16[1024,1024]{1,0:T(8,128)(2,1)} async-done(((bf16[32,1024]{1,0:T(8,128)(2,1)}), bf16[1024,1024]{1,0:T(8,128)(2,1)}) %all-gather.18.cloned.1.call-update) | async-done | bytes 2097168 | tf_op jit(solution)/shard_map/all_gather | solution.py:310
  348.1 75.7 %all-gather.20.cloned.1.call-done = bf16[1024,4096]{1,0:T(8,128)(2,1)} async-done(((bf16[32,4096]{1,0:T(8,128)(2,1)}), bf16[1024,4096]{1,0:T(8,128)(2,1)}) %all-gather.20.cloned.1.call-update) | async-done | bytes 8388624 | tf_op jit(solution)/shard_map/all_gather | solution.py:311
  423.8 6.2 convolution_add_fusion.3
  432.7 70.1 %all-gather.22.cloned.1.call-done = bf16[4096,1024]{1,0:T(8,128)(2,1)} async-done(((bf16[128,1024]{1,0:T(8,128)(2,1)}), bf16[4096,1024]{1,0:T(8,128)(2,1)}) %all-gather.22.cloned.1.call-update) | async-done | bytes 8388624 | tf_op jit(solution)/shard_map/all_gather | solution.py:312
  502.8 11.3 convert_reduce_fusion
  514.2 6.8 fusion.125
  521.0 8.1 convert_reduce_fusion.1
  540.0 32.8 %while.58 = (s32[]{:T(128)}, f32[1,128,8,128]{1,3,2,0:T(8,128)}, bf16[2,512,1,2048]{3,1,0,2:T(8,128)(2,1)}, s32[2]{0:T(128)S(1)}, bf16[1,1024,1024]{1,2,0:T(8,12...) while((s32[]{:T(128)}, f32[1,128,8,128]{1,3,2,0:T(8,128)}, ...), condition=%wide.region_19.20_spmd.clone, body=%wide.region_18.19_spmd.clone.sunk | while | flops 680460288 | bytes 45235016 | solution.py:231
  579.1 32.9 %while.59 = (s32[]{:T(128)}, f32[1,128,8,128]{1,3,2,0:T(8,128)}, bf16[2,512,1,2048]{3,1,0,2:T(8,128)(2,1)}, s32[2]{0:T(128)S(1)}, bf16[1,1024,1024]{1,2,0:T(8,12...) while((s32[]{:T(128)}, f32[1,128,8,128]{1,3,2,0:T(8,128)}, ...), condition=%wide.region_26.27_spmd.clone, body=%wide.region_25.26_spmd.clone.sunk | while | flops 680460288 | bytes 46283612 | solution.py:231
  618.0 41.6 %reduce-scatter.7.cloned.1.call-done = bf16[128,1,2048]{2,0,1:T(8,128)(2,1)} async-done(((bf16[1024,1,2048]{2,0,1:T(8,128)(2,1)}), bf16[128,1,2048]{2,0,1:T(8,128)(2,1)}) %reduce-scatter.7.cloned.1.call-update) | async-done | bytes 524304 | tf_op jit(solution)/shard_map/reduce_scatter | solution.py:234
  659.7 7.4 fusion.85
  667.1 84.3 %reduce-scatter.9.cloned.1.call-done = bf16[128,1,2048]{2,0,1:T(8,128)(2,1)} async-done(((bf16[1024,1,2048]{2,0,1:T(8,128)(2,1)}), bf16[128,1,2048]{2,0,1:T(8,128)(2,1)}) %reduce-scatter.9.cloned.1.call-update) | async-done | bytes 524304 | tf_op jit(solution)/shard_map/reduce_scatter | solution.py:234
  751.4 11.1 convolution_add_fusion.2
  767.3 8.2 convolution_add_fusion.1
  776.6 11.1 fusion.92
  787.7 13.3 convolution_add_fusion
  801.8 9.6 fusion.47
  811.5 8.2 fusion.49
  825.6 43.2 %all-reduce.13 = (f32[1024]{0:T(1024)S(1)}, f32[1024]{0:T(1024)S(1)}, f32[1024]{0:T(1024)S(1)}, f32[1024]{0:T(1024)S(1)}, f32[1024]{0:T(1024)S(1)}, /*index=5*/f32[4096]{0:T(1024)S(1)}, f32[1024]{0:T(1024)S(1)}) all-reduce(f32[1024]{0:T(1024)S(1)} %add.307, ...), channel_id=25, replica_groups=mesh['batch'=4,'blk'=8] {'batch','blk'}, use_global_device_ids=true, to_apply=%region_39.40.clone | all-reduce | flops 10240 | bytes 81920
  874.5 23.8 %reduce-scatter.13.cloned.1.call-done = f32[32,1024]{1,0:T(8,128)} async-done(((f32[1024,1024]{1,0:T(8,128)}), f32[32,1024]{1,0:T(8,128)}) %reduce-scatter.13.cloned.1.call-update) | async-done | bytes 131088 | tf_op jit(solution)/shard_map/reduce_scatter | solution.py:328
  898.2 159.0 %reduce-scatter.11.cloned.1.call-done = f32[32,3072]{1,0:T(8,128)} async-done(((f32[1024,3072]{1,0:T(8,128)}), f32[32,3072]{1,0:T(8,128)}) %reduce-scatter.11.cloned.1.call-update) | async-done | bytes 393232 | tf_op jit(solution)/shard_map/reduce_scatter | solution.py:327
  1057.3 360.1 %reduce-scatter.15.cloned.1.call-done = f32[32,4096]{1,0:T(8,128)} async-done(((f32[1024,4096]{1,0:T(8,128)}), f32[32,4096]{1,0:T(8,128)}) %reduce-scatter.15.cloned.1.call-update) | async-done | bytes 524304 | tf_op jit(solution)/shard_map/reduce_scatter | solution.py:329
  1417.4 360.2 %reduce-scatter.17.cloned.1.call-done = f32[128,1024]{1,0:T(8,128)} async-done(((f32[4096,1024]{1,0:T(8,128)}), f32[128,1024]{1,0:T(8,128)}) %reduce-scatter.17.cloned.1.call-update) | async-done | bytes 524304 | tf_op jit(solution)/shard_map/reduce_scatter | solution.py:330
  (436 shorter events, 175.8 us)
Async XLA Ops:
  7.2 76.2 %all-gather.16.cloned.1.call-start = ((), (), s32[]{:S(2)}) async-start(), calls=%async_computation.6 | async-start | bytes 6488064 | tf_op jit(solution)/shard_map/all_gather | solution.py:309
  7.9 192.1 %all-gather.28.cloned.1.call-start = ((), (), s32[]{:S(2)}) async-start(), calls=%async_computation.14 | async-start | bytes 2359296 | tf_op jit(solution)/shard_map/all_gather | solution.py:133
  55.4 33.6 %copy-start.49 = (f32[1024]{0:T(1024)}, f32[1024]{0:T(1024)S(1)}, u32[]{:S(2)}) copy-start(f32[1024]{0:T(1024)S(1)} %convert_element_type.199) | copy-start | bytes 12292
  55.4 33.6 %copy-start.47 = (f32[1024]{0:T(1024)}, f32[1024]{0:T(1024)S(1)}, u32[]{:S(2)}) copy-start(f32[1024]{0:T(1024)S(1)} %convert_element_type.198) | copy-start | bytes 12292
  88.3 115.7 %all-gather.30.cloned.1.call-start = ((), (), s32[]{:S(2)}) async-start(), calls=%async_computation.15 | async-start | bytes 2359296 | tf_op jit(solution)/shard_map/all_gather | solution.py:134
  89.0 147.9 %all-gather.24.cloned.1.call-start = ((), (), s32[]{:S(2)}) async-start(), calls=%async_computation.12 | async-start | bytes 2359296 | tf_op jit(solution)/shard_map/all_gather | solution.py:133
  93.0 69.5 %copy-start.79 = (s32[2,1,128]{2,1,0:T(1,128)S(1)}, s32[2,1,128]{2,1,0:T(1,128)}, u32[]{:S(2)}) copy-start(s32[2,1,128]{2,1,0:T(1,128)} %param.23) | copy-start | bytes 3076
  93.9 192.7 %all-gather.26.cloned.1.call-start = ((), (), s32[]{:S(2)}) async-start(), calls=%async_computation.13 | async-start | bytes 2359296 | tf_op jit(solution)/shard_map/all_gather | solution.py:134
  94.5 250.0 %all-gather.18.cloned.1.call-start = ((), (), s32[]{:S(2)}) async-start(), calls=%async_computation.7 | async-start | bytes 2162688 | tf_op jit(solution)/shard_map/all_gather | solution.py:310
  95.1 328.7 %all-gather.20.cloned.1.call-start = ((), (), s32[]{:S(2)}) async-start(), calls=%async_computation.8 | async-start | bytes 8650752 | tf_op jit(solution)/shard_map/all_gather | solution.py:311
  95.8 407.0 %all-gather.22.cloned.1.call-start = ((), (), s32[]{:S(2)}) async-start(), calls=%async_computation.9 | async-start | bytes 8650752 | tf_op jit(solution)/shard_map/all_gather | solution.py:312
  96.6 563.1 %reduce-scatter.7.cloned.1.call-start = ((), (), s32[]{:S(2)}) async-start(), calls=%async_computation.10 | async-start | bytes 4718592 | tf_op jit(solution)/shard_map/reduce_scatter | solution.py:234
  162.5 267.5 %copy-start.51 = (f32[1024]{0:T(1024)}, f32[1024]{0:T(1024)S(1)}, u32[]{:S(2)}) copy-start(f32[1024]{0:T(1024)S(1)} %convert_element_type.207) | copy-start | bytes 12292
  304.3 42.8 %copy-start.32 = (f32[1,8,128,128]{2,3,1,0:T(8,128)}, f32[1,8,128,128]{2,3,1,0:T(8,128)S(1)}, u32[]{:S(2)}) copy-start(f32[1,8,128,128]{2,3,1,0:T(8,128)S(1)} %copy.122) | copy-start | bytes 1572868
  305.6 41.5 %copy-start.39 = (bf16[1,8,128,128]{2,3,1,0:T(8,128)(2,1)}, bf16[1,8,128,128]{2,3,1,0:T(8,128)(2,1)S(1)}, u32[]{:S(2)}) copy-start(bf16[1,8,128,128]{2,3,1,0:T(8,128)(2,1)S(1)} %fusion.99) | copy-start | bytes 786436
  346.8 185.9 %copy-start.7 = (f32[128,1024]{1,0:T(8,128)}, f32[128,1024]{1,0:T(8,128)S(1)}, u32[]{:S(2)}) copy-start(f32[128,1024]{1,0:T(8,128)S(1)} %get-tuple-element.699) | copy-start | bytes 1572868
  347.8 184.9 %copy-start.12 = (f32[128,1024]{1,0:T(8,128)}, f32[128,1024]{1,0:T(8,128)S(1)}, u32[]{:S(2)}) copy-start(f32[128,1024]{1,0:T(8,128)S(1)} %get-tuple-element.701) | copy-start | bytes 1572868
  572.9 178.5 %reduce-scatter.9.cloned.1.call-start = ((), (), s32[]{:S(2)}) async-start(), calls=%async_computation.11 | async-start | bytes 4718592 | tf_op jit(solution)/shard_map/reduce_scatter | solution.py:234
  612.0 286.2 %reduce-scatter.13.cloned.1.call-start = ((), (), s32[]{:S(2)}) async-start(), calls=%async_computation.17 | async-start | bytes 4325376 | tf_op jit(solution)/shard_map/reduce_scatter | solution.py:328
  616.6 43.1 %copy-start.11 = (bf16[2,1,128,1024]{3,2,1,0:T(8,128)(2,1)S(1)}, bf16[2,1,128,1024]{3,2,1,0:T(8,128)(2,1)}, u32[]{:S(2)}) copy-start(bf16[2,1,128,1024]{3,2,1,0:T(8,128)(2,1)} %param.22) | copy-start | bytes 1572868
  616.6 43.0 %copy-start.48 = (f32[1024]{0:T(1024)S(1)}, f32[1024]{0:T(1024)}, u32[]{:S(2)}) copy-start(f32[1024]{0:T(1024)} %copy-done.47) | copy-start | bytes 12292
  616.6 43.0 %copy-start.50 = (f32[1024]{0:T(1024)S(1)}, f32[1024]{0:T(1024)}, u32[]{:S(2)}) copy-start(f32[1024]{0:T(1024)} %copy-done.49) | copy-start | bytes 12292
  616.6 43.0 %copy-start.61 = (f32[128]{0:T(128)S(1)}, f32[128]{0:T(128)}, u32[]{:S(2)}) copy-start(f32[128]{0:T(128)} %copy-done.60) | copy-start | bytes 1540
  616.6 43.0 %copy-start.76 = (f32[128]{0:T(128)S(1)}, f32[128]{0:T(128)}, u32[]{:S(2)}) copy-start(f32[128]{0:T(128)} %copy-done.75) | copy-start | bytes 1540
  616.7 440.6 %reduce-scatter.11.cloned.1.call-start = ((), (), s32[]{:S(2)}) async-start(), calls=%async_computation.16 | async-start | bytes 12976128 | tf_op jit(solution)/shard_map/reduce_scatter | solution.py:327
  618.0 49.1 %copy-start.53 = (bf16[128,1024]{1,0:T(8,128)(2,1)}, bf16[128,1024]{1,0:T(8,128)(2,1)S(1)}, u32[]{:S(2)}) copy-start(bf16[128,1024]{1,0:T(8,128)(2,1)S(1)} %copy.172) | copy-start | bytes 786436
  659.7 91.7 %copy-start.59 = (f32[128]{0:T(128)S(1)}, f32[128]{0:T(128)}, u32[]{:S(2)}) copy-start(f32[128]{0:T(128)} %copy-done.58) | copy-start | bytes 1540
  659.7 91.7 %copy-start.74 = (f32[128]{0:T(128)S(1)}, f32[128]{0:T(128)}, u32[]{:S(2)}) copy-start(f32[128]{0:T(128)} %copy-done.73) | copy-start | bytes 1540
  762.6 654.8 %reduce-scatter.15.cloned.1.call-start = ((), (), s32[]{:S(2)}) async-start(), calls=%async_computation.18 | async-start | bytes 17301504 | tf_op jit(solution)/shard_map/reduce_scatter | solution.py:329
  775.5 1002.1 %reduce-scatter.17.cloned.1.call-start = ((), (), s32[]{:S(2)}) async-start(), calls=%async_computation.19 | async-start | bytes 17301504 | tf_op jit(solution)/shard_map/reduce_scatter | solution.py:330
  823.1 49.8 %copy-start.27 = (f32[128,1024]{1,0:T(8,128)S(1)}, f32[128,1024]{1,0:T(8,128)}, u32[]{:S(2)}) copy-start(f32[128,1024]{1,0:T(8,128)} %get-tuple-element.689) | copy-start | bytes 1572868
  823.2 49.8 %copy-start.30 = (f32[128,1024]{1,0:T(8,128)S(1)}, f32[128,1024]{1,0:T(8,128)}, u32[]{:S(2)}) copy-start(f32[128,1024]{1,0:T(8,128)} %copy-done.28) | copy-start | bytes 1572868
  (80 other events, 306.5 us)
Sparse Core Ops, SparseCore 0:
  11.0 72.3 all-gather.15
  88.4 47.8 all-gather.27
  139.0 47.8 all-gather.29
  188.9 47.9 all-gather.23
  238.8 47.7 all-gather.25
  289.5 55.0 all-gather.17
  347.5 76.2 all-gather.19
  426.8 75.9 all-gather.21
  573.0 86.6 reduce-scatter.6
  663.6 87.7 reduce-scatter.8
  754.3 143.9 reduce-scatter.12
  904.7 152.5 reduce-scatter.10
  1060.2 357.1 reduce-scatter.14
  1420.2 357.3 reduce-scatter.16
where the time goes:
time: 1790 us; the launch traced here: 1780 us
  waiting for transfers between devices  1300 us (73%)
  blocking collectives  186 us (10%)
  matrix products  164 us (9%)
  local copies, waits for them, and re-layouts  90.7 us (5%)
    reduce_scatter x1, waiting for transfers between devices, body(): lax.psum_scatter(local_grads[3], ('batch', 'blk'), scatter_dimension=0, t...  360 us
    reduce_scatter x1, waiting for transfers between devices, body(): lax.psum_scatter(local_grads[2], ('batch', 'blk'), scatter_dimension=0, t...  360 us
    reduce_scatter x1, waiting for transfers between devices, body(): lax.psum_scatter(local_grads[0], ('batch', 'blk'), scatter_dimension=0, t...  159 us
    reduce_scatter x2, waiting for transfers between devices, micro_step(): lax.psum_scatter(terms.reshape(length, set_count, 2 * features).astype(jn...  126 us
    unnamed x2, blocking collectives  85.6 us
    all_gather x1, waiting for transfers between devices, body(): lax.all_gather(up_weight, ('batch', 'blk'), axis=0, tiled=True)  75.7 us
    all_gather x1, waiting for transfers between devices, body(): lax.all_gather(down_weight, ('batch', 'blk'), axis=0, tiled=True)  70.1 us
    all_gather x1, blocking collectives, body(): lax.all_gather(up_bias, ('batch', 'blk'), axis=0, tiled=True)  65.8 us
  transfers between devices with their start and end apart: 14, of which 12 were waited for; matrix products, arithmetic and copies ran while one was open for 10% of the time, Pallas kernels for 0%

commit v1 on v0

--- a/solution.py
+++ b/solution.py
@@ -3,6 +3,8 @@
 import jax
 import jax.numpy as jnp
 from jax import lax
+from jax.experimental import pallas as pl
+from jax.experimental.pallas import tpu as pltpu
 from jax.sharding import PartitionSpec as P
 
 H = 8
@@ -340,9 +342,341 @@
     return (jnp.stack(outcomes), jnp.stack(input_grads)) + tuple(shard_sums)
 
 
+AXES = ("batch", "blk")
+Y, C, ZH, Z0, X = 16, 8, 4, 2, 1
+TEAM = (0, Z0, C, C | Z0)
+
+
+def swap(values, mask):
+    return lax.ppermute(values, AXES, [(i, i ^ mask) for i in range(32)])
+
+
+def regroup(values, flip):
+    pairs = []
+    for i in range(32):
+        core, right = (i >> 3) & 1, i & 1
+        pairs.append((i, (i & (Y | Z0)) | (right << 3) | ((i & ZH) ^ (flip << 2)) | core))
+    return lax.ppermute(values, AXES, pairs)
+
+
+def ordered(near, far, bit, axis):
+    return jnp.stack((jnp.where(bit == 0, near, far), jnp.where(bit == 0, far, near)), axis)
+
+
+def grow(values, axis, bit, mask):
+    return ordered(values, swap(values, mask), bit, axis)
+
+
+def pick(values, place, axis=0):
+    return lax.dynamic_index_in_dim(values, place, axis, keepdims=False)
+
+
+def shrink(values, axis, bit, mask):
+    got = swap(pick(values, 1 - bit, axis), mask)
+    return pick(values, bit, axis).astype(jnp.float32) + got.astype(jnp.float32)
+
+
+def low(values):
+    return values.astype(jnp.bfloat16)
+
+
+def wide(values):
+    return values.astype(jnp.float32)
+
+
+def team_trade(parts, quarter, bit_c, bit_z):
+    own = pick(parts, quarter)
+    got = [swap(pick(parts, quarter ^ r), TEAM[r]) for r in (1, 2, 3)]
+    return ordered(
+        ordered(own, got[0], bit_z, 0), ordered(got[1], got[2], bit_z, 0), bit_c, 0
+    )
+
+
+def team_gather(rows):
+    near = jnp.concatenate((rows, swap(rows, Z0)), 0)
+    return jnp.concatenate((near, swap(near, C)), 0)
+
+
+def team_scatter(near, far):
+    half = near.shape[0] // 2
+    near = wide(near) + wide(swap(low(far), C))
+    return near[:half] + wide(swap(low(near[half:]), Z0))
+
+
+def dot_t(former, latter):
+    return lax.dot_general(
+        former, latter, (((1,), (1,)), ((), ())), preferred_element_type=jnp.float32
+    )
+
+
+def dot_rows(former, latter):
+    return lax.dot_general(
+        former, latter, (((0,), (0,)), ((), ())), preferred_element_type=jnp.float32
+    )
+
+
+STEP = 256
+HEAD = 128
+
+
+def attend_kernel(seg_col, seg_row, mixed, out, logs):
+    rows = mixed.shape[0]
+    heads = out.shape[1] // HEAD
+    scale = HEAD ** (-0.5)
+    for head in range(heads):
+        at_q, at_k, at_v = (HEAD * (part * heads + head) for part in range(3))
+
+        def block(number, unused):
+            spot = pl.ds(pl.multiple_of(number * STEP, STEP), STEP)
+            scores = dot_t(mixed[:, at_k : at_k + HEAD], mixed[spot, at_q : at_q + HEAD]) * scale
+            scores = jnp.where(seg_col[...] == seg_row[:, spot], scores, masked_score)
+            highest = jnp.max(scores, axis=0, keepdims=True)
+            shares = jnp.exp(scores - highest)
+            total = jnp.sum(shares, axis=0, keepdims=True)
+            mixture = dot_rows(mixed[:, at_v : at_v + HEAD], low(shares)) / total
+            out[spot, at_q : at_q + HEAD] = low(mixture.T)
+            logs[head : head + 1, spot] = highest + jnp.log(total)
+            return unused
+
+        lax.fori_loop(0, rows // STEP, block, 0)
+
+
+def attend_back_kernel(seg_col, seg_row, mixed, grads, logs, out, key_sum, value_sum):
+    rows = mixed.shape[0]
+    heads = grads.shape[1] // HEAD
+    scale = HEAD ** (-0.5)
+    for head in range(heads):
+        at_q, at_k, at_v = (HEAD * (part * heads + head) for part in range(3))
+        key_sum[...] = jnp.zeros_like(key_sum)
+        value_sum[...] = jnp.zeros_like(value_sum)
+
+        def block(number, unused):
+            spot = pl.ds(pl.multiple_of(number * STEP, STEP), STEP)
+            queries = mixed[spot, at_q : at_q + HEAD]
+            grad = grads[spot, at_q : at_q + HEAD]
+            keys = mixed[:, at_k : at_k + HEAD]
+            scores = dot_t(keys, queries) * scale
+            shares = jnp.exp(scores - logs[head : head + 1, spot])
+            shares = jnp.where(seg_col[...] == seg_row[:, spot], shares, 0.0)
+            grad_shares = dot_t(mixed[:, at_v : at_v + HEAD], grad)
+            delta = jnp.sum(shares * grad_shares, axis=0, keepdims=True)
+            grad_scores = low(shares * (grad_shares - delta))
+            value_sum[...] += jnp.dot(low(shares), grad, preferred_element_type=jnp.float32)
+            key_sum[...] += jnp.dot(grad_scores, queries, preferred_element_type=jnp.float32)
+            out[spot, at_q : at_q + HEAD] = low((dot_rows(keys, grad_scores) * scale).T)
+            return unused
+
+        lax.fori_loop(0, rows // STEP, block, 0)
+        out[:, at_k : at_k + HEAD] = low(key_sum[...] * scale)
+        out[:, at_v : at_v + HEAD] = low(value_sum[...])
+
+
+def attend(seg_col, seg_row, mixed):
+    rows, columns = mixed.shape
+    heads = columns // (3 * HEAD)
+    work = 2 * rows * rows * HEAD * heads
+    return pl.pallas_call(
+        attend_kernel,
+        out_shape=(
+            jax.ShapeDtypeStruct((rows, heads * HEAD), jnp.bfloat16),
+            jax.ShapeDtypeStruct((heads, rows), jnp.float32),
+        ),
+        compiler_params=pltpu.CompilerParams(vmem_limit_bytes=24 << 20),
+        cost_estimate=pl.CostEstimate(
+            flops=2 * work, transcendentals=rows * rows * heads, bytes_accessed=4 << 20
+        ),
+        name="attend",
+    )(seg_col, seg_row, mixed)
+
+
+def attend_back(seg_col, seg_row, mixed, grads, logs):
+    rows, columns = mixed.shape
+    heads = columns // (3 * HEAD)
+    work = 2 * rows * rows * HEAD * heads
+    return pl.pallas_call(
+        attend_back_kernel,
+        out_shape=jax.ShapeDtypeStruct((rows, columns), jnp.bfloat16),
+        scratch_shapes=[pltpu.VMEM((rows, HEAD), jnp.float32)] * 2,
+        compiler_params=pltpu.CompilerParams(vmem_limit_bytes=32 << 20),
+        cost_estimate=pl.CostEstimate(
+            flops=5 * work, transcendentals=rows * rows * heads, bytes_accessed=6 << 20
+        ),
+        name="attend_back",
+    )(seg_col, seg_row, mixed, grads, logs)
+
+
+def team_body(
+    inputs,
+    segment_ids,
+    cotangent,
+    qkv_weight,
+    out_weight,
+    up_weight,
+    down_weight,
+    first_gain,
+    first_bias,
+    second_gain,
+    second_bias,
+    out_bias,
+    up_bias,
+    down_bias,
+):
+    batch_at, blk_at = lax.axis_index("batch"), lax.axis_index("blk")
+    y, c = batch_at >> 1, batch_at & 1
+    zh, z0, x = blk_at >> 2, (blk_at >> 1) & 1, blk_at & 1
+    quarter = 2 * c + z0
+    tokens, features = inputs.shape[2:]
+    own_rows = 2 * tokens
+
+    packed = jnp.concatenate(
+        (
+            first_gain,
+            first_bias,
+            second_gain,
+            second_bias,
+            out_bias,
+            down_bias,
+            up_bias,
+            low(segment_ids.reshape(-1)),
+        )
+    )[None]
+    for bit, mask in ((c, C), (x, X), (z0, Z0), (y, Y), (zh, ZH)):
+        axis = {C: 0, X: 1, Z0: 1, Y: 0, ZH: 2}[mask]
+        packed = grow(packed, axis, bit, mask)
+    packed = packed.reshape(32, -1)
+    vectors = wide(packed[:, :192]).reshape(32, 6, 32).transpose(1, 0, 2).reshape(6, features)
+    gain_one, shift_one, gain_two, shift_two, bias_out, bias_down = vectors
+    bias_up = wide(packed[:, 192:320]).reshape(2, 2, 2, 2, 2, 128)
+    bias_up = pick(pick(bias_up, z0, 3), c, 1).reshape(-1)
+    ids = wide(packed[:, 320:]).reshape(2, 2, 8, 2, tokens)
+    ids = pick(pick(pick(ids, y), x), zh, 1)
+    row = jnp.arange(8)
+    chunk = 4 * ((row & 1) ^ zh) + 2 * (((row >> 1) & 1) ^ z0) + ((row >> 2) ^ c)
+    same = chunk[:, None] == jnp.arange(8)[None, :]
+    ids = jnp.sum(jnp.where(same[:, :, None], ids[None], 0.0), axis=1)
+    seg_row = ids.reshape(1, -1)
+    seg_col = ids.reshape(-1, 1)
+
+    qkv_parts = qkv_weight.reshape(32, 6, 4, 128).transpose(2, 0, 1, 3).reshape(4, 32, 768)
+    up_parts = up_weight.reshape(32, 2, 2, 2, 2, 2, 128).transpose(2, 4, 0, 1, 3, 5, 6)
+    up_parts = up_parts.reshape(4, 32, 1024)
+    parts = team_trade(jnp.concatenate((qkv_parts, up_parts), 2), quarter, c, z0)
+    w_qkv = parts[..., :768]
+    w_qkv = grow(grow(grow(w_qkv, 1, zh, ZH), 3, x, X), 0, y, Y).reshape(features, -1)
+    w_out = grow(out_weight, 0, z0, Z0)
+    w_out = jnp.where(zh == z0, w_out, swap(w_out, ZH))
+    w_out = grow(grow(w_out, 1, x, X), 0, y, Y).reshape(-1, features)
+    w_up = grow(grow(grow(parts[..., 768:], 1, zh, ZH), 0, y, Y), 4, x, X).reshape(features, -1)
+    w_down = grow(grow(grow(down_weight, 0, zh, ZH), 1, x, X), 0, y, Y).reshape(-1, features)
+
+    def take_rows(values):
+        return jnp.concatenate(
+            [regroup(pick(values[:, 0], zh ^ flip), flip) for flip in (0, 1)], 0
+        )
+
+    def give_rows(values):
+        near = regroup(low(values[:tokens]), 0)
+        far = regroup(low(values[tokens:]), 1)
+        return wide(ordered(near, far, zh, 0))[:, None]
+
+    rows = wide(take_rows(inputs))
+    normed, scaled_one, inverse_one = norm_rows(rows, gain_one, shift_one)
+    normed = team_gather(low(normed))
+    mixed = low(dense(normed, w_qkv))
+    attended, logs = attend(seg_col, seg_row, mixed)
+    half = attended.shape[0] // 2
+
+    def split_dense(former, product):
+        return team_scatter(product(former[:half]), product(former[half:]))
+
+    middle = rows + split_dense(attended, lambda v: dense(v, w_out)) + bias_out
+    normed_two, scaled_two, inverse_two = norm_rows(middle, gain_two, shift_two)
+    normed_two = team_gather(low(normed_two))
+    upper = dense(normed_two, w_up) + bias_up
+    activ, gelu_back = jax.vjp(lambda v: jax.nn.gelu(v, approximate=False), upper)
+    activ = low(activ)
+    grad_own = take_rows(cotangent)
+    grad_out = team_gather(grad_own)
+    grad_own = wide(grad_own)
+    grad_upper = low(gelu_back(dot_t(grad_out, w_down))[0])
+    grad_two = split_dense(grad_upper, lambda v: dot_t(v, w_up))
+    final = give_rows(middle + split_dense(activ, lambda v: dense(v, w_down)) + bias_down)
+
+    grad_down = low(dot_rows(activ, grad_out)).reshape(2, 2, 2, 128, features)
+    grad_down = shrink(low(shrink(low(shrink(grad_down, 0, y, Y)), 1, x, X)), 0, zh, ZH)
+    grad_up = low(dot_rows(normed_two, grad_upper)).reshape(2, 2, 2, 2, 2, 32, -1)
+    grad_up = shrink(low(shrink(low(shrink(grad_up, 4, x, X)), 0, y, Y)), 1, zh, ZH)
+    grad_up = team_trade(low(grad_up).reshape(4, 32, -1), quarter, c, z0)
+    grad_up = grad_up.reshape(2, 2, 32, 2, 2, 2, 128).transpose(2, 3, 0, 4, 1, 5, 6)
+    grad_up = wide(grad_up.reshape(32, -1))
+
+    grad_middle = grad_own + norm_back(grad_two, scaled_two, inverse_two, gain_two)
+    branch_own = low(grad_middle)
+    branch = team_gather(branch_own)
+    grad_attended = low(dot_t(branch, w_out))
+    grad_w_out = low(dot_rows(attended, branch)).reshape(2, 2, 2, 32, features)
+    grad_w_out = low(shrink(low(shrink(grad_w_out, 0, y, Y)), 1, x, X))
+    grad_w_out = wide(grad_w_out) + wide(swap(grad_w_out, ZH))
+    handed = swap(low(pick(grad_w_out, 1 - z0)), Z0)
+    grad_w_out = jnp.where(zh == z0, pick(grad_w_out, z0), wide(handed))
+
+    grad_mixed = attend_back(seg_col, seg_row, mixed, grad_attended, logs)
+    grad_one = split_dense(grad_mixed, lambda v: dot_t(v, w_qkv))
+    grad_qkv = low(dot_rows(normed, grad_mixed)).reshape(2, 2, 2, 2, 2, 32, -1)
+    grad_qkv = shrink(low(shrink(low(shrink(grad_qkv, 0, y, Y)), 3, x, X)), 1, zh, ZH)
+    grad_qkv = team_trade(low(grad_qkv).reshape(4, 32, -1), quarter, c, z0)
+    grad_qkv = wide(grad_qkv.reshape(4, 32, 6, 128).transpose(1, 2, 0, 3).reshape(32, -1))
+    input_grad = give_rows(
+        grad_middle + norm_back(grad_one, scaled_one, inverse_one, gain_one)
+    )
+
+    sums = jnp.stack(
+        (
+            jnp.sum(grad_one * scaled_one, 0),
+            jnp.sum(grad_one, 0),
+            jnp.sum(grad_two * scaled_two, 0),
+            jnp.sum(grad_two, 0),
+            jnp.sum(wide(branch_own), 0),
+            jnp.sum(grad_own, 0),
+        )
+    )
+    up_sums = jnp.sum(wide(grad_upper), 0)
+    spread = jnp.where(jnp.arange(4)[:, None] == quarter, up_sums[None], 0.0)
+    sums = jnp.concatenate((sums, spread), 0)
+    for mask in (C, X, Z0, Y, ZH):
+        sums = sums + swap(sums, mask)
+    flat = batch_at * 8 + blk_at
+    small = lax.dynamic_slice_in_dim(sums[:6], flat * 32, 32, 1)
+    grad_up_bias = pick(sums[6:], quarter)
+    grad_up_bias = lax.dynamic_slice_in_dim(grad_up_bias, (4 * y + 2 * zh + x) * 128, 128)
+    return (
+        final,
+        input_grad,
+        grad_qkv,
+        grad_w_out,
+        grad_up,
+        grad_down,
+        small[0],
+        small[1],
+        small[2],
+        small[3],
+        small[4],
+        grad_up_bias,
+        small[5],
+    )
+
+
+def chosen_body(mesh, *arrays):
+    shape = arrays[0].shape
+    sizes = (mesh.shape["batch"], mesh.shape["blk"])
+    if sizes == (4, 8) and shape == (2, 1, 128, 1024) and arrays[5].shape == (32, 4096):
+        return team_body(*arrays)
+    return body(*arrays)
+
+
 def solution(mesh):
     return jax.shard_map(
-        body,
+        partial(chosen_body, mesh),
         mesh=mesh,
         in_specs=(
             P(None, "batch", "blk", None),

time: 1790 us -> 419 us (0.23)
  waiting for transfers between devices: 1300 us -> 223 us
  blocking collectives: 186 us -> 0 us
  matrix products: 164 us -> 40 us
  starting transfers between devices: 1.17 us -> 61.3 us
  local copies, waits for them, and re-layouts: 90.7 us -> 33.8 us
  other arithmetic: 17.5 us -> 36.5 us
    reduce_scatter x6 -> x0, waiting for transfers between devices: 1030 us -> none  [the longest x1 360 us: body(): lax.psum_scatter(local_grads[3], ('batch', 'blk'), scatter_dimension=0, t...]
    all_gather x8 -> x0, waiting for transfers between devices: 270 us -> none  [the longest x1 75.7 us: body(): lax.all_gather(up_weight, ('batch', 'blk'), axis=0, tiled=True)]
    ppermute x0 -> x69, waiting for transfers between devices: none -> 223 us  [the longest x61 212 us: swap(): return lax.ppermute(values, AXES, [(i, i ^ mask) for i in range(32)])]
    all_gather x3 -> x0, blocking collectives: 101 us -> none  [the longest x1 65.8 us: body(): lax.all_gather(up_bias, ('batch', 'blk'), axis=0, tiled=True)]
    dot_general x44 -> x10, matrix products: 126 us -> 30.1 us  [the longest x6 18.9 us: dot_t(): lax.dot_general(former, latter, (((1,), (1,)), ((), ())), preferred_eleme...]
    unnamed x2 -> x0, blocking collectives: 85.6 us -> none
    ppermute x0 -> x69, starting transfers between devices: none -> 61.3 us  [the longest x61 51.2 us: swap(): return lax.ppermute(values, AXES, [(i, i ^ mask) for i in range(32)])]
    unnamed x183 -> x83, local copies, waits for them, and re-layouts: 36.2 us -> 8.66 us
  transfers between devices with their start and end apart: 14 -> 69, of which waited for: 12 -> 33; matrix products, arithmetic and copies ran while one was open for 10% -> 19% of each run, Pallas kernels for 0% -> 4%
where the time goes in v1:
time: 419 us; the launch traced here: 413 us
  waiting for transfers between devices  223 us (53%)
  starting transfers between devices  61.3 us (15%)
  matrix products  40 us (10%)
  other arithmetic  36.5 us (9%)
  local copies, waits for them, and re-layouts  33.8 us (8%)
  Pallas kernels  15.7 us (4%)
    ppermute x61, waiting for transfers between devices, swap(): return lax.ppermute(values, AXES, [(i, i ^ mask) for i in range(32)])  212 us
    ppermute x61, starting transfers between devices, swap(): return lax.ppermute(values, AXES, [(i, i ^ mask) for i in range(32)])  51.2 us
    dot_general x6, matrix products, dot_t(): lax.dot_general(former, latter, (((1,), (1,)), ((), ())), preferred_eleme...  18.9 us
    another operation x42, other arithmetic, ordered(): jnp.stack((jnp.where(bit == 0, near, far), jnp.where(bit == 0, far, near)...  11.8 us
    dot_general x4, matrix products, dot_rows(): lax.dot_general(former, latter, (((0,), (0,)), ((), ())), preferred_eleme...  11.1 us
    ppermute x8, waiting for transfers between devices, regroup(): return lax.ppermute(values, AXES, pairs)  10.6 us
    ppermute x8, starting transfers between devices, regroup(): return lax.ppermute(values, AXES, pairs)  10.2 us
    dot_general x6, matrix products, dense(): return jnp.dot(former, latter, preferred_element_type=jnp.float32)  9.97 us
  transfers between devices with their start and end apart: 69, of which 33 were waited for; matrix products, arithmetic and copies ran while one was open for 19% of the time, Pallas kernels for 4%

profile of v1, /device:TPU:0, one launch (start us, length us, event | category | flops | bytes accessed | tf_op | source)
XLA Modules:
  0.0 412.6 jit_solution(5904542040293278281)
XLA Ops:
  1.3 4.8 %concatenate.148 = bf16[576]{0:T(1024)(128)(2,1)S(1)} concatenate(bf16[32]{0:T(256)(128)(2,1)} %param.21, bf16[32]{0:T(256)(128)(2,1)} %param.22, bf16[32]{0:T(256)(128)(2,1)} %param.23, bf16[32]{0:T(256)(128)(2,1)} %param.24, bf16[32]{0:T(256)(128)(2,1)} %param.25, bf16[32]{0:T(256)(128)(2,1)} %param.27, bf16[128]{0:T(256)(128)(2,1)} %param.26, bf16[256]{0:T(256)(128)(2,1)S(1)} %bitcast.339), dimensions={0} | concatenate | bytes 2304 | tf_op jit(solution)/shard_map/concatenate | solution.py:531
  19.2 8.9 %collective-permute-done.4 = bf16[2,2,1,576]{3,0,1,2:T(2,128)(2,1)S(1)} collective-permute-done((bf16[2,2,1,576]{3,0,1,2:T(2,128)(2,1)S(1)}, bf16[2,2,1,576]{3,0,1,2:T(2,128)(2,1)S(1)}, u32[]{:S(2)}, u32[]{:S(2)}) %collective-permute-start.4) | collective-permute-done | bytes 4640 | tf_op jit(solution)/shard_map/ppermute | solution.py:351
  32.1 4.6 %collective-permute-done.6 = bf16[2,2,2,2,1,576]{5,1,3,2,4,0:T(2,128)(2,1)S(1)} collective-permute-done((bf16[2,2,2,2,1,576]{5,1,3,2,4,0:T(2,128)(2,1)S(1)}, bf16[2,2,2,2,1,576]{5,1,3,2,4,0:T(2,128)(2,1)S(1)}, u32[]{:S(2)}, u32[]{:S(2)}) %collective-permute-start.6) | collective-permute-done | bytes 18464 | tf_op jit(solution)/shard_map/ppermute | solution.py:351
  38.3 3.0 collective-permute-start.34
  41.5 28.2 %collective-permute-done.16 = bf16[2,32,1024]{2,1,0:T(8,128)(2,1)S(1)} collective-permute-done((bf16[2,32,1024]{2,1,0:T(8,128)(2,1)S(1)}, bf16[2,32,1024]{2,1,0:T(8,128)(2,1)S(1)}, u32[]{:S(2)}, u32[]{:S(2)}) %collective-permute-start.16) | collective-permute-done | bytes 131104 | tf_op jit(solution)/shard_map/ppermute | solution.py:351
  70.5 10.1 %collective-permute-done.12 = bf16[2,2,32,768]{3,2,1,0:T(8,128)(2,1)S(1)} collective-permute-done((bf16[2,2,32,768]{3,2,1,0:T(8,128)(2,1)S(1)}, bf16[2,2,32,768]{3,2,1,0:T(8,128)(2,1)S(1)}, u32[]{:S(2)}, u32[]{:S(2)}) %collective-permute-start.12) | collective-permute-done | bytes 196640 | tf_op jit(solution)/shard_map/ppermute | solution.py:351
  82.8 9.0 %collective-permute-done.13 = bf16[2,2,2,32,768]{4,3,2,1,0:T(8,128)(2,1)S(1)} collective-permute-done((bf16[2,2,2,32,768]{4,3,2,1,0:T(8,128)(2,1)S(1)}, bf16[2,2,2,32,768]{4,3,2,1,0:T(8,128)(2,1)S(1)}, u32[]{:S(2)}, u32[]{:S(2)}) %collective-permute-start.13) | collective-permute-done | bytes 393248 | tf_op jit(solution)/shard_map/ppermute | solution.py:351
  100.2 11.6 %collective-permute-done.14 = bf16[2,2,2,2,32,768]{5,4,3,2,1,0:T(8,128)(2,1)} collective-permute-done((bf16[2,2,2,2,32,768]{5,4,3,2,1,0:T(8,128)(2,1)}, bf16[2,2,2,2,32,768]{5,4,3,2,1,0:T(8,128)(2,1)}, u32[]{:S(2)}, u32[]{:S(2)}) %collective-permute-start.14) | collective-permute-done | bytes 786464 | tf_op jit(solution)/shard_map/ppermute | solution.py:351
  114.1 3.0 convolution_convert_fusion.3.mixed
  117.2 6.8 %attend.1 = (bf16[1024,256]{1,0:T(8,128)(2,1)S(1)}, f32[2,1024]{1,0:T(2,128)S(1)}) custom-call(f32[1024,1]{1,0:T(8,128)S(1)} %copy.108.seg_col, f32[1,1024]{1,0:T(1,128)S(1)} %bitcast.299, bf16[1024,768]{1,0:T(8,128)(2,1)S(1)} %convolution_convert_fusion.3.mixed), custom_call_target="tpu_custom_call" | custom-call | flops 1073741824 | bytes 4194304 | tf_op jit(solution)/shard_map/attend/pallas_call | solution.py:478
  131.9 7.9 %collective-permute-done.23 = bf16[2,2,32,1024]{3,2,1,0:T(8,128)(2,1)S(1)} collective-permute-done((bf16[2,2,32,1024]{3,2,1,0:T(8,128)(2,1)S(1)}, bf16[2,2,32,1024]{3,2,1,0:T(8,128)(2,1)S(1)}, u32[]{:S(2)}, u32[]{:S(2)}) %collective-permute-start.23) | collective-permute-done | bytes 262176 | tf_op jit(solution)/shard_map/ppermute | solution.py:351
  143.9 6.2 %collective-permute-done.35 = bf16[256,1024]{1,0:T(8,128)(2,1)S(1)} collective-permute-done((bf16[256,1024]{1,0:T(8,128)(2,1)S(1)}, bf16[256,1024]{1,0:T(8,128)(2,1)S(1)}, u32[]{:S(2)}, u32[]{:S(2)}) %collective-permute-start.35) | collective-permute-done | bytes 524320 | tf_op jit(solution)/shard_map/ppermute | solution.py:351
  152.3 8.4 %collective-permute-done.20 = bf16[256,1024]{1,0:T(8,128)(2,1)S(1)} collective-permute-done((bf16[256,1024]{1,0:T(8,128)(2,1)S(1)}, bf16[256,1024]{1,0:T(8,128)(2,1)S(1)}, u32[]{:S(2)}, u32[]{:S(2)}) %collective-permute-start.20) | collective-permute-done | bytes 524320 | tf_op jit(solution)/shard_map/ppermute | solution.py:351
  167.8 8.1 %collective-permute-done.21 = bf16[256,1024]{1,0:T(8,128)(2,1)} collective-permute-done((bf16[256,1024]{1,0:T(8,128)(2,1)}, bf16[256,1024]{1,0:T(8,128)(2,1)}, u32[]{:S(2)}, u32[]{:S(2)}) %collective-permute-start.21) | collective-permute-done | bytes 524320 | tf_op jit(solution)/shard_map/ppermute | solution.py:351
  181.8 7.3 %collective-permute-done.25 = bf16[2,2,2,2,32,1024]{5,4,3,1,2,0:T(8,128)(2,1)} collective-permute-done((bf16[2,2,2,2,32,1024]{5,4,3,1,2,0:T(8,128)(2,1)}, bf16[2,2,2,2,32,1024]{5,4,3,1,2,0:T(8,128)(2,1)}, u32[]{:S(2)}, u32[]{:S(2)}) %collective-permute-start.25) | collective-permute-done | bytes 1048608 | tf_op jit(solution)/shard_map/ppermute | solution.py:351
  191.0 3.5 fusion.40
  194.5 12.4 %convert_reduce_fusion = (f32[1024]{0:T(1024)S(1)}, bf16[1024,1024]{1,0:T(8,128)(2,1)S(1)}, f32[1024,1024]{1,0:T(8,128)S(1)}) fusion(f32[1024,1024]{1,0:T(8,128)S(1)} %fusion.40, f32[1024]{0:T(1024)S(1)} %bitcast.330, bf16[1024,1024]{1,0:T(8,128)(2,1)S(1)} %constant_dynamic-update-slice_fusion.4, bf16[1024,1024]{1,0:T(8,128)(2,1)S(1)} %bitcast.308), kind=kOutput, calls=%fused_computation.2 | convolution fusion | flops 2226125824 | bytes 14688256 | tf_op jit(solution)/shard_map/dot_general | solution.py:407
  209.4 3.6 convolution_convert_fusion.1
  224.4 14.4 %collective-permute-done.55 = bf16[2,2,2,2,32,1024]{5,4,3,2,1,0:T(8,128)(2,1)S(1)} collective-permute-done((bf16[2,2,2,2,32,1024]{5,4,3,2,1,0:T(8,128)(2,1)S(1)}, bf16[2,2,2,2,32,1024]{5,4,3,2,1,0:T(8,128)(2,1)S(1)}, u32[]{:S(2)}, u32[]{:S(2)}) %collective-permute-start.55) | collective-permute-done | bytes 1048608 | tf_op jit(solution)/shard_map/ppermute | solution.py:351
  246.2 9.5 %collective-permute-done.56 = bf16[2,2,2,32,1024]{4,3,2,1,0:T(8,128)(2,1)S(1)} collective-permute-done((bf16[2,2,2,32,1024]{4,3,2,1,0:T(8,128)(2,1)S(1)}, bf16[2,2,2,32,1024]{4,3,2,1,0:T(8,128)(2,1)S(1)}, u32[]{:S(2)}, u32[]{:S(2)}) %collective-permute-start.56) | collective-permute-done | bytes 524320 | tf_op jit(solution)/shard_map/ppermute | solution.py:351
  267.0 4.6 %collective-permute-done.57 = bf16[2,2,32,1024]{3,2,1,0:T(8,128)(2,1)S(1)} collective-permute-done((bf16[2,2,32,1024]{3,2,1,0:T(8,128)(2,1)S(1)}, bf16[2,2,32,1024]{3,2,1,0:T(8,128)(2,1)S(1)}, u32[]{:S(2)}, u32[]{:S(2)}) %collective-permute-start.57) | collective-permute-done | bytes 262176 | tf_op jit(solution)/shard_map/ppermute | solution.py:351
  271.7 15.3 %collective-permute-done.39 = bf16[256,1024]{1,0:T(8,128)(2,1)S(1)} collective-permute-done((bf16[256,1024]{1,0:T(8,128)(2,1)S(1)}, bf16[256,1024]{1,0:T(8,128)(2,1)S(1)}, u32[]{:S(2)}, u32[]{:S(2)}) %collective-permute-start.39) | collective-permute-done | bytes 524320 | tf_op jit(solution)/shard_map/ppermute | solution.py:351
  305.8 8.9 %attend_back.1 = bf16[1024,768]{1,0:T(8,128)(2,1)S(1)} custom-call(f32[1024,1]{1,0:T(8,128)S(1)} %copy.108.seg_col, f32[1,1024]{1,0:T(1,128)S(1)} %bitcast.300, bf16[1024,768]{1,0:T(8,128)(2,1)S(1)} %copy-done.1, bf16[1024,256]{1,0:T(8,128)(2,1)S(1)} %convolution_convert_fusion.9.grads, f32[2,1024]{1,0:T(2,128)S(1)} %get-tuple-element.16.logs), custom_call_target="tpu_custom_call" | custom-call | flops 2684354560 | bytes 6291456 | tf_op jit(solution)/shard_map/attend_back/pallas_call | solution.py:496
  314.7 3.1 convolution_convert_fusion.2
  322.4 3.2 collective-permute-done.52
  327.9 10.7 %collective-permute-done.45 = bf16[2,2,2,2,32,768]{5,4,3,2,1,0:T(8,128)(2,1)} collective-permute-done((bf16[2,2,2,2,32,768]{5,4,3,2,1,0:T(8,128)(2,1)}, bf16[2,2,2,2,32,768]{5,4,3,2,1,0:T(8,128)(2,1)}, u32[]{:S(2)}, u32[]{:S(2)}) %collective-permute-start.45) | collective-permute-done | bytes 786464 | tf_op jit(solution)/shard_map/ppermute | solution.py:351
  342.9 7.6 %collective-permute-done.46 = bf16[2,2,2,32,768]{4,3,2,1,0:T(8,128)(2,1)S(1)} collective-permute-done((bf16[2,2,2,32,768]{4,3,2,1,0:T(8,128)(2,1)S(1)}, bf16[2,2,2,32,768]{4,3,2,1,0:T(8,128)(2,1)S(1)}, u32[]{:S(2)}, u32[]{:S(2)}) %collective-permute-start.46) | collective-permute-done | bytes 393248 | tf_op jit(solution)/shard_map/ppermute | solution.py:351
  352.3 8.6 %collective-permute-done.47 = bf16[2,2,32,768]{3,2,1,0:T(8,128)(2,1)S(1)} collective-permute-done((bf16[2,2,32,768]{3,2,1,0:T(8,128)(2,1)S(1)}, bf16[2,2,32,768]{3,2,1,0:T(8,128)(2,1)S(1)}, u32[]{:S(2)}, u32[]{:S(2)}) %collective-permute-start.47) | collective-permute-done | bytes 196640 | tf_op jit(solution)/shard_map/ppermute | solution.py:351
  365.6 10.3 %collective-permute-done.50 = bf16[32,768]{1,0:T(8,128)(2,1)S(1)} collective-permute-done((bf16[32,768]{1,0:T(8,128)(2,1)S(1)}, bf16[32,768]{1,0:T(8,128)(2,1)S(1)}, u32[]{:S(2)}, u32[]{:S(2)}) %collective-permute-start.50) | collective-permute-done | bytes 49184 | tf_op jit(solution)/shard_map/ppermute | solution.py:351
  379.9 3.6 collective-permute-done.65
  384.8 3.1 collective-permute-done.66
  398.7 10.6 %collective-permute-done.44 = bf16[128,1024]{1,0:T(8,128)(2,1)S(1)} collective-permute-done((bf16[128,1024]{1,0:T(8,128)(2,1)S(1)}, bf16[128,1024]{1,0:T(8,128)(2,1)S(1)}, u32[]{:S(2)}, u32[]{:S(2)}) %collective-permute-start.44) | collective-permute-done | bytes 262176 | tf_op jit(solution)/shard_map/ppermute | solution.py:359
  (377 shorter events, 149.3 us)
Async XLA Ops:
  6.6 30.9 %collective-permute-start.15 = (bf16[32,1024]{1,0:T(8,128)(2,1)}, bf16[32,1024]{1,0:T(8,128)(2,1)S(1)}, u32[]{:S(2)}, u32[]{:S(2)}) collective-permute-start(bf16[32,1024]{1,0:T(8,128)(2,1)} %param.18), channel_id=1, source_target_pairs={{0,2},{1,3},{2,0},{3,1},{4,6},{5,7},{6,4},{7,5},{8,10},{9,11},{10,... | collective-permute-start | bytes 196616 | tf_op jit(solution)/shard_map/ppermute | solution.py:351
  9.3 115.4 %collective-permute-start.26 = (bf16[128,1024]{1,0:T(8,128)(2,1)}, bf16[128,1024]{1,0:T(8,128)(2,1)}, u32[]{:S(2)}, u32[]{:S(2)}) collective-permute-start(bf16[128,1024]{1,0:T(8,128)(2,1)} %param.20), channel_id=1, source_target_pairs={{0,4},{1,5},{2,6},{3,7},{4,0},{5,1},{6,2},{7,3},{8,12},{9,13},{10,... | collective-permute-start | bytes 786440 | tf_op jit(solution)/shard_map/ppermute | solution.py:351
  16.5 21.7 %collective-permute-start.9 = (bf16[32,1792]{1,0:T(8,128)(2,1)S(1)}, bf16[32,1792]{1,0:T(8,128)(2,1)S(1)}, u32[]{:S(2)}, u32[]{:S(2)}) collective-permute-start(bf16[32,1792]{1,0:T(8,128)(2,1)S(1)} %get-tuple-element.79), channel_id=1, source_target_pairs={{0,2},{1,3},{2,0},{3,1},{4,6},{5,7},{6,4},{7,5},{8,10},{9,11},{10,... | collective-permute-start | bytes 344072 | tf_op jit(solution)/shard_map/ppermute | solution.py:351
  17.0 21.3 %collective-permute-start.11 = (bf16[32,1792]{1,0:T(8,128)(2,1)S(1)}, bf16[32,1792]{1,0:T(8,128)(2,1)S(1)}, u32[]{:S(2)}, u32[]{:S(2)}) collective-permute-start(bf16[32,1792]{1,0:T(8,128)(2,1)S(1)} %get-tuple-element.80), channel_id=1, source_target_pairs={{0,10},{1,11},{2,8},{3,9},{4,14},{5,15},{6,12},{7,13},{8,2},{9,3},... | collective-permute-start | bytes 344072 | tf_op jit(solution)/shard_map/ppermute | solution.py:351
  37.5 32.3 %collective-permute-start = (bf16[128,1024]{1,0:T(8,128)(2,1)S(1)}, bf16[128,1024]{1,0:T(8,128)(2,1)S(1)}, u32[]{:S(2)}, u32[]{:S(2)}) collective-permute-start(bf16[128,1024]{1,0:T(8,128)(2,1)S(1)} %get-tuple-element.73), channel_id=1, source_target_pairs={{0,0},{1,8},{2,2},{3,10},{4,4},{5,12},{6,6},{7,14},{8,1},{9,9},{10... | collective-permute-start | bytes 786440 | tf_op jit(solution)/shard_map/ppermute | solution.py:359
  38.2 31.8 %collective-permute-start.1 = (bf16[128,1024]{1,0:T(8,128)(2,1)S(1)}, bf16[128,1024]{1,0:T(8,128)(2,1)S(1)}, u32[]{:S(2)}, u32[]{:S(2)}) collective-permute-start(bf16[128,1024]{1,0:T(8,128)(2,1)S(1)} %get-tuple-element.74), channel_id=1, source_target_pairs={{0,4},{1,12},{2,6},{3,14},{4,0},{5,8},{6,2},{7,10},{8,5},{9,13},{1... | collective-permute-start | bytes 786440 | tf_op jit(solution)/shard_map/ppermute | solution.py:359
  38.3 89.1 %collective-permute-start.34 = (bf16[128,1024]{1,0:T(8,128)(2,1)}, bf16[128,1024]{1,0:T(8,128)(2,1)}, u32[]{:S(2)}, u32[]{:S(2)}) collective-permute-start(bf16[128,1024]{1,0:T(8,128)(2,1)} %get-tuple-element.69), channel_id=1, source_target_pairs={{0,4},{1,12},{2,6},{3,14},{4,0},{5,8},{6,2},{7,10},{8,5},{9,13},{1... | collective-permute-start | bytes 786440 | tf_op jit(solution)/shard_map/ppermute | solution.py:359
  41.3 28.4 %collective-permute-start.16 = (bf16[2,32,1024]{2,1,0:T(8,128)(2,1)S(1)}, bf16[2,32,1024]{2,1,0:T(8,128)(2,1)S(1)}, u32[]{:S(2)}, u32[]{:S(2)}) collective-permute-start(bf16[2,32,1024]{2,1,0:T(8,128)(2,1)S(1)} %pad_maximum_fusion.29), channel_id=1, source_target_pairs={{0,4},{1,5},{2,6},{3,7},{4,0},{5,1},{6,2},{7,3},{8,12},{9,13},{10,... | collective-permute-start | bytes 393224 | tf_op jit(solution)/shard_map/ppermute | solution.py:351
  92.8 18.9 %collective-permute-start.14 = (bf16[2,2,2,2,32,768]{5,4,3,2,1,0:T(8,128)(2,1)}, bf16[2,2,2,2,32,768]{5,4,3,2,1,0:T(8,128)(2,1)}, u32[]{:S(2)}, u32[]{:S(2)}) collective-permute-start(bf16[2,2,2,2,32,768]{5,4,3,2,1,0:T(8,128)(2,1)} %pad_maximum_fusion.18), channel_id=1, source_target_pairs={{0,16},{1,17},{2,18},{3,19},{4,20},{5,21},{6,22},{7,23},{8,24},{9,... | collective-permute-start | bytes 2359304 | tf_op jit(solution)/shard_map/ppermute | solution.py:351
  96.8 16.5 %collective-permute-start.8 = (bf16[512,1024]{1,0:T(8,128)(2,1)}, bf16[512,1024]{1,0:T(8,128)(2,1)}, u32[]{:S(2)}, u32[]{:S(2)}) collective-permute-start(bf16[512,1024]{1,0:T(8,128)(2,1)} %pad_maximum_fusion.6), channel_id=1, source_target_pairs={{0,8},{1,9},{2,10},{3,11},{4,12},{5,13},{6,14},{7,15},{8,0},{9,1},... | collective-permute-start | bytes 3145736 | tf_op jit(solution)/shard_map/ppermute | solution.py:351
  97.5 29.2 %collective-permute-start.33 = (bf16[128,1024]{1,0:T(8,128)(2,1)}, bf16[128,1024]{1,0:T(8,128)(2,1)S(1)}, u32[]{:S(2)}, u32[]{:S(2)}) collective-permute-start(bf16[128,1024]{1,0:T(8,128)(2,1)} %get-tuple-element.70), channel_id=1, source_target_pairs={{0,0},{1,8},{2,2},{3,10},{4,4},{5,12},{6,6},{7,14},{8,1},{9,9},{10... | collective-permute-start | bytes 786440 | tf_op jit(solution)/shard_map/ppermute | solution.py:359
  124.5 17.0 %collective-permute-start.19 = (bf16[512,1024]{1,0:T(8,128)(2,1)S(1)}, bf16[512,1024]{1,0:T(8,128)(2,1)S(1)}, u32[]{:S(2)}, u32[]{:S(2)}) collective-permute-start(bf16[512,1024]{1,0:T(8,128)(2,1)S(1)} %convolution_convert_fusion.7), channel_id=1, source_target_pairs={{0,8},{1,9},{2,10},{3,11},{4,12},{5,13},{6,14},{7,15},{8,0},{9,1},... | collective-permute-start | bytes 3145736 | tf_op jit(solution)/shard_map/ppermute | solution.py:351
  129.2 20.9 %collective-permute-start.35 = (bf16[256,1024]{1,0:T(8,128)(2,1)S(1)}, bf16[256,1024]{1,0:T(8,128)(2,1)S(1)}, u32[]{:S(2)}, u32[]{:S(2)}) collective-permute-start(bf16[256,1024]{1,0:T(8,128)(2,1)S(1)} %get-tuple-element.91), channel_id=1, source_target_pairs={{0,2},{1,3},{2,0},{3,1},{4,6},{5,7},{6,4},{7,5},{8,10},{9,11},{10,... | collective-permute-start | bytes 1572872 | tf_op jit(solution)/shard_map/ppermute | solution.py:351
  139.9 22.4 %collective-permute-start.24 = (bf16[2,2,2,32,1024]{4,3,2,0,1:T(8,128)(2,1)S(1)}, bf16[2,2,2,32,1024]{4,3,2,0,1:T(8,128)(2,1)S(1)}, u32[]{:S(2)}, u32[]{:S(2)}) collective-permute-start(bf16[2,2,2,32,1024]{4,3,2,0,1:T(8,128)(2,1)S(1)} %pad_maximum_fusion.21), channel_id=1, source_target_pairs={{0,16},{1,17},{2,18},{3,19},{4,20},{5,21},{6,22},{7,23},{8,24},{9,... | collective-permute-start | bytes 1572872 | tf_op jit(solution)/shard_map/ppermute | solution.py:351
  142.1 18.6 %collective-permute-start.20 = (bf16[256,1024]{1,0:T(8,128)(2,1)S(1)}, bf16[256,1024]{1,0:T(8,128)(2,1)S(1)}, u32[]{:S(2)}, u32[]{:S(2)}) collective-permute-start(bf16[256,1024]{1,0:T(8,128)(2,1)S(1)} %slice.239), channel_id=1, source_target_pairs={{0,2},{1,3},{2,0},{3,1},{4,6},{5,7},{6,4},{7,5},{8,10},{9,11},{10,... | collective-permute-start | bytes 1572872 | tf_op jit(solution)/shard_map/ppermute | solution.py:351
  143.4 33.9 %collective-permute-start.28 = (bf16[2,2,128,1024]{3,2,0,1:T(8,128)(2,1)}, bf16[2,2,128,1024]{3,2,0,1:T(8,128)(2,1)}, u32[]{:S(2)}, u32[]{:S(2)}) collective-permute-start(bf16[2,2,128,1024]{3,2,0,1:T(8,128)(2,1)} %pad_maximum_fusion.9), channel_id=1, source_target_pairs={{0,16},{1,17},{2,18},{3,19},{4,20},{5,21},{6,22},{7,23},{8,24},{9,... | collective-permute-start | bytes 3145736 | tf_op jit(solution)/shard_map/ppermute | solution.py:351
  152.3 26.9 %collective-permute-start.36 = (bf16[512,1024]{1,0:T(8,128)(2,1)}, bf16[512,1024]{1,0:T(8,128)(2,1)}, u32[]{:S(2)}, u32[]{:S(2)}) collective-permute-start(bf16[512,1024]{1,0:T(8,128)(2,1)} %pad_maximum_fusion.10), channel_id=1, source_target_pairs={{0,8},{1,9},{2,10},{3,11},{4,12},{5,13},{6,14},{7,15},{8,0},{9,1},... | collective-permute-start | bytes 3145736 | tf_op jit(solution)/shard_map/ppermute | solution.py:351
  164.2 24.9 %collective-permute-start.25 = (bf16[2,2,2,2,32,1024]{5,4,3,1,2,0:T(8,128)(2,1)}, bf16[2,2,2,2,32,1024]{5,4,3,1,2,0:T(8,128)(2,1)}, u32[]{:S(2)}, u32[]{:S(2)}) collective-permute-start(bf16[2,2,2,2,32,1024]{5,4,3,1,2,0:T(8,128)(2,1)} %pad_maximum_fusion.8), channel_id=1, source_target_pairs={{0,1},{1,0},{2,3},{3,2},{4,5},{5,4},{6,7},{7,6},{8,9},{9,8},{10,11... | collective-permute-start | bytes 3145736 | tf_op jit(solution)/shard_map/ppermute | solution.py:351
  213.2 25.6 %collective-permute-start.55 = (bf16[2,2,2,2,32,1024]{5,4,3,2,1,0:T(8,128)(2,1)S(1)}, bf16[2,2,2,2,32,1024]{5,4,3,2,1,0:T(8,128)(2,1)S(1)}, u32[]{:S(2)}, u32[]{:S(2)}) collective-permute-start(bf16[2,2,2,2,32,1024]{5,4,3,2,1,0:T(8,128)(2,1)S(1)} %dynamic-slice_bitcast_fusion), channel_id=1, source_target_pairs={{0,1},{1,0},{2,3},{3,2},{4,5},{5,4},{6,7},{7,6},{8,9},{9,8},{10,11... | collective-permute-start | bytes 3145736 | tf_op jit(solution)/shard_map/ppermute | solution.py:351
  218.4 22.5 %collective-permute-start.29 = (bf16[512,1024]{1,0:T(8,128)(2,1)S(1)}, bf16[512,1024]{1,0:T(8,128)(2,1)S(1)}, u32[]{:S(2)}, u32[]{:S(2)}) collective-permute-start(bf16[512,1024]{1,0:T(8,128)(2,1)S(1)} %convolution_convert_fusion.6), channel_id=1, source_target_pairs={{0,8},{1,9},{2,10},{3,11},{4,12},{5,13},{6,14},{7,15},{8,0},{9,1},... | collective-permute-start | bytes 3145736 | tf_op jit(solution)/shard_map/ppermute | solution.py:351
  219.0 26.0 %collective-permute-start.61 = (bf16[2,2,128,1024]{3,2,0,1:T(8,128)(2,1)S(1)}, bf16[2,2,128,1024]{3,2,0,1:T(8,128)(2,1)S(1)}, u32[]{:S(2)}, u32[]{:S(2)}) collective-permute-start(bf16[2,2,128,1024]{3,2,0,1:T(8,128)(2,1)S(1)} %bitcast.320), channel_id=1, source_target_pairs={{0,16},{1,17},{2,18},{3,19},{4,20},{5,21},{6,22},{7,23},{8,24},{9,... | collective-permute-start | bytes 3145736 | tf_op jit(solution)/shard_map/ppermute | solution.py:351
  222.6 35.1 %collective-permute-start.38 = (bf16[256,1024]{1,0:T(8,128)(2,1)S(1)}, bf16[256,1024]{1,0:T(8,128)(2,1)S(1)}, u32[]{:S(2)}, u32[]{:S(2)}) collective-permute-start(bf16[256,1024]{1,0:T(8,128)(2,1)S(1)} %slice.237), channel_id=1, source_target_pairs={{0,2},{1,3},{2,0},{3,1},{4,6},{5,7},{6,4},{7,5},{8,10},{9,11},{10,... | collective-permute-start | bytes 1572872 | tf_op jit(solution)/shard_map/ppermute | solution.py:351
  239.3 16.4 %collective-permute-start.56 = (bf16[2,2,2,32,1024]{4,3,2,1,0:T(8,128)(2,1)S(1)}, bf16[2,2,2,32,1024]{4,3,2,1,0:T(8,128)(2,1)S(1)}, u32[]{:S(2)}, u32[]{:S(2)}) collective-permute-start(bf16[2,2,2,32,1024]{4,3,2,1,0:T(8,128)(2,1)S(1)} %dynamic-slice_bitcast_fusion.3), channel_id=1, source_target_pairs={{0,16},{1,17},{2,18},{3,19},{4,20},{5,21},{6,22},{7,23},{8,24},{9,... | collective-permute-start | bytes 1572872 | tf_op jit(solution)/shard_map/ppermute | solution.py:351
  242.2 16.8 %collective-permute-start.30 = (bf16[256,1024]{1,0:T(8,128)(2,1)S(1)}, bf16[256,1024]{1,0:T(8,128)(2,1)S(1)}, u32[]{:S(2)}, u32[]{:S(2)}) collective-permute-start(bf16[256,1024]{1,0:T(8,128)(2,1)S(1)} %slice.238), channel_id=1, source_target_pairs={{0,2},{1,3},{2,0},{3,1},{4,6},{5,7},{6,4},{7,5},{8,10},{9,11},{10,... | collective-permute-start | bytes 1572872 | tf_op jit(solution)/shard_map/ppermute | solution.py:351
  245.5 18.6 %collective-permute-start.62 = (bf16[2,128,1024]{2,1,0:T(8,128)(2,1)S(1)}, bf16[2,128,1024]{2,1,0:T(8,128)(2,1)S(1)}, u32[]{:S(2)}, u32[]{:S(2)}) collective-permute-start(bf16[2,128,1024]{2,1,0:T(8,128)(2,1)S(1)} %dynamic-slice_bitcast_fusion.2), channel_id=1, source_target_pairs={{0,1},{1,0},{2,3},{3,2},{4,5},{5,4},{6,7},{7,6},{8,9},{9,8},{10,11... | collective-permute-start | bytes 1572872 | tf_op jit(solution)/shard_map/ppermute | solution.py:351
  262.2 136.5 %collective-permute-start.31 = (bf16[128,1024]{1,0:T(8,128)(2,1)}, bf16[128,1024]{1,0:T(8,128)(2,1)S(1)}, u32[]{:S(2)}, u32[]{:S(2)}) collective-permute-start(bf16[128,1024]{1,0:T(8,128)(2,1)} %get-tuple-element.65), channel_id=1, source_target_pairs={{0,0},{1,8},{2,2},{3,10},{4,4},{5,12},{6,6},{7,14},{8,1},{9,9},{10... | collective-permute-start | bytes 786440 | tf_op jit(solution)/shard_map/ppermute | solution.py:359
  263.8 23.2 %collective-permute-start.39 = (bf16[256,1024]{1,0:T(8,128)(2,1)S(1)}, bf16[256,1024]{1,0:T(8,128)(2,1)S(1)}, u32[]{:S(2)}, u32[]{:S(2)}) collective-permute-start(bf16[256,1024]{1,0:T(8,128)(2,1)S(1)} %get-tuple-element.35), channel_id=1, source_target_pairs={{0,2},{1,3},{2,0},{3,1},{4,6},{5,7},{6,4},{7,5},{8,10},{9,11},{10,... | collective-permute-start | bytes 1572872 | tf_op jit(solution)/shard_map/ppermute | solution.py:351
  264.4 25.7 %collective-permute-start.63 = (bf16[128,1024]{1,0:T(8,128)(2,1)S(1)}, bf16[128,1024]{1,0:T(8,128)(2,1)S(1)}, u32[]{:S(2)}, u32[]{:S(2)}) collective-permute-start(bf16[128,1024]{1,0:T(8,128)(2,1)S(1)} %dynamic-slice_bitcast_fusion.5), channel_id=1, source_target_pairs={{0,4},{1,5},{2,6},{3,7},{4,0},{5,1},{6,2},{7,3},{8,12},{9,13},{10,... | collective-permute-start | bytes 786440 | tf_op jit(solution)/shard_map/ppermute | solution.py:351
  293.1 105.6 %collective-permute-start.32 = (bf16[128,1024]{1,0:T(8,128)(2,1)}, bf16[128,1024]{1,0:T(8,128)(2,1)}, u32[]{:S(2)}, u32[]{:S(2)}) collective-permute-start(bf16[128,1024]{1,0:T(8,128)(2,1)} %get-tuple-element.66), channel_id=1, source_target_pairs={{0,4},{1,12},{2,6},{3,14},{4,0},{5,8},{6,2},{7,10},{8,5},{9,13},{1... | collective-permute-start | bytes 786440 | tf_op jit(solution)/shard_map/ppermute | solution.py:359
  302.2 17.2 %collective-permute-start.51 = (bf16[2,2,32,1024]{3,2,0,1:T(8,128)(2,1)S(1)}, bf16[2,2,32,1024]{3,2,0,1:T(8,128)(2,1)S(1)}, u32[]{:S(2)}, u32[]{:S(2)}) collective-permute-start(bf16[2,2,32,1024]{3,2,0,1:T(8,128)(2,1)S(1)} %bitcast.328), channel_id=1, source_target_pairs={{0,16},{1,17},{2,18},{3,19},{4,20},{5,21},{6,22},{7,23},{8,24},{9,... | collective-permute-start | bytes 786440 | tf_op jit(solution)/shard_map/ppermute | solution.py:351
  318.9 19.8 %collective-permute-start.45 = (bf16[2,2,2,2,32,768]{5,4,3,2,1,0:T(8,128)(2,1)}, bf16[2,2,2,2,32,768]{5,4,3,2,1,0:T(8,128)(2,1)}, u32[]{:S(2)}, u32[]{:S(2)}) collective-permute-start(bf16[2,2,2,2,32,768]{5,4,3,2,1,0:T(8,128)(2,1)} %dynamic-slice_bitcast_fusion.1), channel_id=1, source_target_pairs={{0,16},{1,17},{2,18},{3,19},{4,20},{5,21},{6,22},{7,23},{8,24},{9,... | collective-permute-start | bytes 2359304 | tf_op jit(solution)/shard_map/ppermute | solution.py:351
  341.4 19.6 %collective-permute-start.41 = (bf16[512,1024]{1,0:T(8,128)(2,1)S(1)}, bf16[512,1024]{1,0:T(8,128)(2,1)S(1)}, u32[]{:S(2)}, u32[]{:S(2)}) collective-permute-start(bf16[512,1024]{1,0:T(8,128)(2,1)S(1)} %convolution_convert_fusion.4), channel_id=1, source_target_pairs={{0,8},{1,9},{2,10},{3,11},{4,12},{5,13},{6,14},{7,15},{8,0},{9,1},... | collective-permute-start | bytes 3145736 | tf_op jit(solution)/shard_map/ppermute | solution.py:351
  (76 other events, 788.7 us)
